TPU v7x, 256 devices: a whole 4x4x8 slice. The times are simulated.
256 devices in a mesh: section: 16 (over y_hi, x, core), ray: 8 (over z), dp: 2 (over y_lo).
Axes of the slice: x: 4, y: 4 (y_hi: 2, y_lo: 2; y = y_hi * 2 + y_lo), z: 8, core: 2. Of those that a mesh axis runs over, the one named last changes fastest.
Arguments:
- section_tokens: bfloat16 [16, 2, 1024, 1024], P('section', 'dp', 'ray'), may hold values from -6 to 6
- enc_ln1: float32 [16, 1024], P('section'), may hold values from 0.5 to 1.5
- enc_qkv: bfloat16 [16, 1024, 3, 1024], P('section', None, None, 'ray'), may hold values from -40 to 40
- enc_out: bfloat16 [16, 1024, 1024], P('section', 'ray'), may hold values from -0.1875 to 0.1875
- enc_ln2: float32 [16, 1024], P('section'), may hold values from 0.5 to 1.5
- enc_up: bfloat16 [16, 1024, 4096], P('section', None, 'ray'), may hold values from -0.1875 to 0.1875
- enc_down: bfloat16 [16, 4096, 1024], P('section', 'ray'), may hold values from -0.09375 to 0.09375
- set_latent: bfloat16 [2, 1024, 1024], P('dp', 'ray'), may hold values from -6 to 6
- ray_queries: bfloat16 [2, 32768, 1024], P('dp', ('section', 'ray')), may hold values from -6 to 6
- dec_query: bfloat16 [1024, 1024], P('section'), may hold values from -40 to 40
- dec_kv: bfloat16 [1024, 2, 1024], P('section'), may hold values from -1 to 1
- dec_out: bfloat16 [1024, 1024], P('section'), may hold values from -0.1875 to 0.1875
- feature_grad: bfloat16 [2, 32768, 1024], P('dp', ('section', 'ray')), may hold values from -2 to 2
Outputs:
- handed: bfloat16 [16, 2, 1024, 1024], P('section', 'dp', 'ray')
- finished: bfloat16 [2, 1024, 1024], P('dp', 'ray', 'section')
- ray_features: bfloat16 [2, 32768, 1024], P('dp', ('section', 'ray'))
- latent_grad: bfloat16 [2, 1024, 1024], P('dp', 'ray')
- out_grad: float32 [1024, 1024], replicated
All inputs are finite; a program needn't handle non-finite values.
Results may differ from a plain program's by a relative error of at most 0.022.
The roundings to bfloat16 on the way count: a program that leaves them out, or rounds other values in their place, can miss the bound.
Values may be sent and summed in bfloat16 or wider, within the bound.
No kernel may reach another device: no remote copies, remote signals or barrier semaphores. Data moves between devices by JAX's collectives and lax.ppermute only.
A program may use at most 128 MiB of HBM per device.

v0:
```python
import math
import jax
import jax.numpy as jnp
from jax import lax
from jax.sharding import PartitionSpec as P

HEADS = 16


def shifted(value, axis, by):
    count = lax.axis_size(axis)
    pairs = [(i, i + by) for i in range(count) if 0 <= i + by < count]
    return lax.ppermute(value, axis, pairs)


def spread_2(value, axis, root):
    mine = lax.axis_index(axis) == root
    return lax.psum(jnp.where(mine, value, jnp.zeros_like(value)), axis)


def layer_norm(values, gain):
    values = values.astype(jnp.float32)
    center = values - jnp.mean(values, -1, keepdims=True)
    spread = jnp.mean(center * center, -1, keepdims=True)
    return center * lax.rsqrt(spread + 1e-05) * gain


def softmax_rows(scores):
    top = jnp.max(scores, -1, keepdims=True)
    expo = jnp.exp(scores - top)
    return expo / jnp.sum(expo, -1, keepdims=True)


def attend_heads(packed, head_dim):
    length = packed.shape[0]
    heads = packed.shape[1] // (3 * head_dim)
    split = packed.reshape(length, 3, heads, head_dim)
    scores = jnp.einsum(
        "qhd,khd->hqk", split[:, 0], split[:, 1], preferred_element_type=jnp.float32
    ) / math.sqrt(head_dim)
    probs = softmax_rows(scores).astype(jnp.bfloat16)
    mixed = jnp.einsum("hqk,khd->qhd", probs, split[:, 2], preferred_element_type=jnp.float32)
    return mixed.astype(jnp.bfloat16).reshape(length, heads * head_dim)


def latent_rows(pair_sum, w_pairs):
    result = lax.dot_general(
        pair_sum[:, 0],
        w_pairs[:, 0, :],
        (((1,), (1,)), ((), ())),
        preferred_element_type=jnp.float32,
    )
    result = result + lax.dot_general(
        pair_sum[:, 1],
        w_pairs[:, 1, :],
        (((1,), (1,)), ((), ())),
        preferred_element_type=jnp.float32,
    )
    return result.astype(jnp.bfloat16)


def local(
    section_tokens,
    enc_ln1,
    enc_qkv,
    enc_out,
    enc_ln2,
    enc_up,
    enc_down,
    set_latent,
    ray_queries,
    dec_query,
    dec_kv,
    dec_out,
    feature_grad,
):
    tokens = section_tokens[0, 0]
    width = tokens.shape[1]
    head_dim = width // HEADS
    local_width = enc_out.shape[1]
    w_qkv = enc_qkv[0].reshape(width, 3 * local_width)
    w_attn_out = enc_out[0]
    w_upper = enc_up[0]
    w_lower = enc_down[0]
    gain_one = enc_ln1[0]
    gain_two = enc_ln2[0]
    normed = layer_norm(tokens, gain_one).astype(jnp.bfloat16)
    packed = jnp.dot(
        lax.all_gather(normed, "ray", axis=0, tiled=True), w_qkv, preferred_element_type=jnp.float32
    ).astype(jnp.bfloat16)
    mixed = attend_heads(packed, head_dim)
    attn_rows = lax.psum_scatter(
        jnp.dot(mixed, w_attn_out, preferred_element_type=jnp.float32).astype(jnp.bfloat16),
        "ray",
        scatter_dimension=0,
        tiled=True,
    ).astype(jnp.float32)
    hidden = (tokens.astype(jnp.float32) + attn_rows).astype(jnp.bfloat16)
    upper = jax.nn.gelu(
        jnp.dot(
            lax.all_gather(
                layer_norm(hidden, gain_two).astype(jnp.bfloat16), "ray", axis=0, tiled=True
            ),
            w_upper,
            preferred_element_type=jnp.float32,
        ),
        approximate=True,
    ).astype(jnp.bfloat16)
    lower_rows = lax.psum_scatter(
        jnp.dot(upper, w_lower, preferred_element_type=jnp.float32).astype(jnp.bfloat16),
        "ray",
        scatter_dimension=0,
        tiled=True,
    ).astype(jnp.float32)
    layer_out = (hidden.astype(jnp.float32) + lower_rows).astype(jnp.bfloat16)
    handed = shifted(layer_out, "section", 1)
    finished_all = spread_2(layer_out, "section", lax.axis_size("section") - 1)
    columns = width // lax.axis_size("section")
    finished = lax.dynamic_slice_in_dim(
        finished_all, lax.axis_index("section") * columns, columns, 1
    )
    w_query, w_pairs, w_mix = (
        lax.all_gather(dec_query, "section", axis=0, tiled=True),
        lax.all_gather(dec_kv, "section", axis=0, tiled=True),
        lax.all_gather(dec_out, "section", axis=0, tiled=True),
    )
    latent = set_latent[0]
    queries = ray_queries[0]
    cotangent = feature_grad[0]
    flat_pairs = w_pairs.reshape(width, 2 * width)
    key_values = lax.all_gather(
        jnp.dot(latent, flat_pairs, preferred_element_type=jnp.float32).astype(jnp.bfloat16),
        "ray",
        axis=0,
        tiled=True,
    )
    scene_len = key_values.shape[0]
    ray_rows = queries.shape[0]
    scale = 1.0 / math.sqrt(head_dim)
    keys = key_values[:, :width].reshape(scene_len, HEADS, head_dim)
    values = key_values[:, width:].reshape(scene_len, HEADS, head_dim)
    query = (
        jnp.dot(queries, w_query, preferred_element_type=jnp.float32)
        .astype(jnp.bfloat16)
        .reshape(ray_rows, HEADS, head_dim)
    )
    scores = jnp.einsum("rhd,lhd->hrl", query, keys, preferred_element_type=jnp.float32) * scale
    probs = softmax_rows(scores)
    probs_low = probs.astype(jnp.bfloat16)
    attended = (
        jnp.einsum("hrl,lhd->rhd", probs_low, values, preferred_element_type=jnp.float32)
        .astype(jnp.bfloat16)
        .reshape(ray_rows, width)
    )
    features = (
        queries.astype(jnp.float32) + jnp.dot(attended, w_mix, preferred_element_type=jnp.float32)
    ).astype(jnp.bfloat16)
    mix_term = lax.dot_general(
        attended, cotangent, (((0,), (0,)), ((), ())), preferred_element_type=jnp.float32
    )
    out_grad = lax.psum(mix_term, ("section", "ray", "dp"))
    attn_grad = lax.dot_general(
        cotangent, w_mix, (((1,), (1,)), ((), ())), preferred_element_type=jnp.float32
    )
    attn_grad = attn_grad.astype(jnp.bfloat16).reshape(ray_rows, HEADS, head_dim)
    prob_grad = jnp.einsum("rhd,lhd->hrl", attn_grad, values, preferred_element_type=jnp.float32)
    delta = jnp.sum(probs * prob_grad, -1, keepdims=True)
    score_grad = (probs * (prob_grad - delta) * scale).astype(jnp.bfloat16)
    count = latent.shape[0] * lax.axis_size("ray")
    key_grad = jnp.einsum(
        "hrl,rhd->lhd", score_grad, query, preferred_element_type=jnp.float32
    ).reshape(count, width)
    value_grad = jnp.einsum(
        "hrl,rhd->lhd", probs_low, attn_grad, preferred_element_type=jnp.float32
    ).reshape(count, width)
    stacked = jnp.stack([key_grad, value_grad], 1)
    pair_rows = lax.psum_scatter(
        stacked.astype(jnp.bfloat16), "ray", scatter_dimension=0, tiled=True
    )
    pair_sum = lax.psum(pair_rows, "section")
    latent_grad = latent_rows(pair_sum, w_pairs)
    return (handed[None, None], finished[None], features[None], latent_grad[None], out_grad)


def solution(mesh):
    return jax.shard_map(
        local,
        mesh=mesh,
        in_specs=(
            P("section", "dp", "ray", None),
            P("section", None),
            P("section", None, None, "ray"),
            P("section", "ray", None),
            P("section", None),
            P("section", None, "ray"),
            P("section", "ray", None),
            P("dp", "ray", None),
            P("dp", ("section", "ray"), None),
            P("section", None),
            P("section", None, None),
            P("section", None),
            P("dp", ("section", "ray"), None),
        ),
        out_specs=(
            P("section", "dp", "ray", None),
            P("dp", "ray", "section"),
            P("dp", ("section", "ray"), None),
            P("dp", "ray", None),
            P(),
        ),
        check_vma=False,
    )
```

profile of v0, /device:TPU:2, one launch (start us, length us, event | category | flops | bytes accessed | tf_op | source)
XLA Modules:
  0.0 928.3 jit_solution(4946242236666145838)
XLA Ops:
  13.8 42.5 %all-gather.7.cloned.1.call-done = bf16[1024,1024]{1,0:T(8,128)(2,1)} async-done(((bf16[128,1024]{1,0:T(8,128)(2,1)}), bf16[1024,1024]{1,0:T(8,128)(2,1)}) %all-gather.7.cloned.1.call-update) | async-done | bytes 2097168 | tf_op jit(solution)/shard_map/all_gather | solution.py:89
  58.9 4.9 fusion.97
  63.7 4.3 fusion.48
  71.9 39.7 %reduce-scatter.6.cloned.1.call-done = bf16[128,1024]{1,0:T(8,128)(2,1)} async-done(((bf16[1024,1024]{1,0:T(8,128)(2,1)}), bf16[128,1024]{1,0:T(8,128)(2,1)}) %reduce-scatter.6.cloned.1.call-update) | async-done | bytes 262160 | tf_op jit(solution)/shard_map/reduce_scatter | solution.py:92
  114.0 18.6 %all-gather.11.cloned.1.call-done = bf16[1024,2,1024]{2,1,0:T(2,128)(2,1)} async-done(((bf16[64,2,1024]{2,1,0:T(2,128)(2,1)}), bf16[1024,2,1024]{2,1,0:T(2,128)(2,1)}) %all-gather.11.cloned.1.call-update) | async-done | bytes 4194320 | tf_op jit(solution)/shard_map/all_gather | solution.py:124
  132.7 11.1 %copy.47 = bf16[1024,2,1024]{0,2,1:T(8,128)(2,1)} copy(bf16[1024,2,1024]{2,1,0:T(2,128)(2,1)} %all-gather.11.cloned.1.call-done) | data formatting | bytes 8388608 | tf_op jit(solution)/shard_map/all_gather | solution.py:124
  143.8 4.6 convolution_convert_fusion
  148.5 39.0 %all-gather.15.cloned.1.call-done = bf16[1024,1024]{1,0:T(8,128)(2,1)} async-done(((bf16[64,1024]{1,0:T(8,128)(2,1)}), bf16[1024,1024]{1,0:T(8,128)(2,1)}) %all-gather.15.cloned.1.call-update) | async-done | bytes 2097168 | tf_op jit(solution)/shard_map/all_gather | solution.py:123
  190.8 51.5 %all-gather.17.cloned.1.call-done = bf16[1024,1024]{1,0:T(8,128)(2,1)} async-done(((bf16[64,1024]{1,0:T(8,128)(2,1)}), bf16[1024,1024]{1,0:T(8,128)(2,1)}) %all-gather.17.cloned.1.call-update) | async-done | bytes 2097168 | tf_op jit(solution)/shard_map/all_gather | solution.py:125
  245.6 39.2 %all-gather.9.cloned.1.call-done = bf16[1024,1024]{1,0:T(8,128)(2,1)} async-done(((bf16[128,1024]{1,0:T(8,128)(2,1)}), bf16[1024,1024]{1,0:T(8,128)(2,1)}) %all-gather.9.cloned.1.call-update) | async-done | bytes 2097168 | tf_op jit(solution)/shard_map/all_gather | solution.py:101
  284.9 5.8 convolution_convert_fusion.1
  290.9 66.2 %all-gather.13.cloned.1.call-done = bf16[1024,2048]{1,0:T(8,128)(2,1)} async-done(((bf16[128,2048]{1,0:T(8,128)(2,1)}), bf16[1024,2048]{1,0:T(8,128)(2,1)}) %all-gather.13.cloned.1.call-update) | async-done | bytes 4194320 | tf_op jit(solution)/shard_map/all_gather | solution.py:131
  366.7 9.8 %fusion.98 = (f32[16,256]{1,0:T(8,128)S(1)}, f32[16,256,1024]{2,1,0:T(8,128)}) fusion(bf16[256,16,64]{0,2,1:T(8,128)(2,1)S(1)} %bitcast.149, bf16[1024,16,64]{0,2,1:T(8,128)(2,1)} %bitcast.144), kind=kOutput, calls=%fused_computation.110 | convolution fusion | flops 549454848 | bytes 19415040 | tf_op jit(solution)/shard_map/sub | solution.py:30
  376.5 8.1 fusion.99
  384.5 38.2 %fusion.38 = bf16[16,64,1024]{2,1,0:T(8,128)(2,1)} fusion(bf16[256,16,64]{0,2,1:T(8,128)(2,1)S(1)} %bitcast.150, f32[16,256,1024]{2,1,0:T(8,128)} %fusion.99, f32[16,256,1024]{2,1,0:T(8,128)} %get-tuple-element.18, f32[16,256]{1,0:T(8,128)S(1)} %get-tuple-element.17), kind=kOutput, calls=%fused_computation.40 | convolution fusion | flops 567284736 | bytes 36192256 | tf_op jit(solution)/shard_map/hrl,rhd->lhd/dot_general | solution.py:170
  422.8 7.1 fusion.35
  432.3 6.5 copy.57
  440.8 52.2 %reduce-scatter.10.cloned.1.call-done = bf16[128,2048]{1,0:T(8,128)(2,1)} async-done(((bf16[1024,2048]{1,0:T(8,128)(2,1)}), bf16[128,2048]{1,0:T(8,128)(2,1)}) %reduce-scatter.10.cloned.1.call-update) | async-done | bytes 524304
  495.3 8.5 fusion.42
  506.5 10.0 %fusion.95 = (bf16[1024,1,1024]{2,1,0:T(2,128)(2,1)}, bf16[1024,1,1024]{2,1,0:T(2,128)(2,1)}) fusion(bf16[1024,2,1024]{2,1,0:T(2,128)(2,1)} %all-gather.11.cloned.1.call-done), kind=kLoop, calls=%fused_computation.107 | loop fusion | bytes 8388608 | tf_op jit(solution)/shard_map/slice | solution.py:49
  520.0 4.7 collective-permute-done
  524.7 109.9 %all-reduce.6.cloned.1.call-done = (bf16[128,1024]{1,0:T(8,128)(2,1)}, bf16[128,2,1024]{0,2,1:T(8,128)(2,1)}) async-done(((bf16[128,1024]{1,0:T(8,128)(2,1)}, bf16[128,2,1024]{0,2,1:T(8,128)(2,1)}), (bf16[128,1024]{1,0:T(8,128)(2,1)}, bf16[128,2,1024]{0,2,1:T(8,128)(2,1)})) %all-reduce.6.cloned.1.call-update) | async-done | bytes 786448 | tf_op jit(solution)/shard_map/psum | solution.py:18
  643.2 272.5 %all-reduce.4.cloned.1.call-done = f32[1024,1024]{1,0:T(8,128)} async-done(((f32[1024,1024]{1,0:T(8,128)}), f32[1024,1024]{1,0:T(8,128)}) %all-reduce.4.cloned.1.call-update) | async-done | bytes 4194320 | tf_op jit(solution)/shard_map/psum | solution.py:161
  916.4 4.8 copy.76
  (84 shorter events, 52.9 us)
Async XLA Ops:
  8.0 276.9 %copy-start = (bf16[1,512,1024]{2,1,0:T(8,128)(2,1)S(1)}, bf16[1,512,1024]{2,1,0:T(8,128)(2,1)}, u32[]{:S(2)}) copy-start(bf16[1,512,1024]{2,1,0:T(8,128)(2,1)} %param.19) | copy-start | bytes 3145732
  8.0 48.2 %all-gather.7.cloned.1.call-start = ((), (), s32[]{:S(2)}) async-start(), calls=%async_computation.3 | async-start | bytes 2359296 | tf_op jit(solution)/shard_map/all_gather | solution.py:89
  12.3 99.4 %reduce-scatter.6.cloned.1.call-start = ((), (), s32[]{:S(2)}) async-start(), calls=%async_computation.4 | async-start | bytes 2359296 | tf_op jit(solution)/shard_map/reduce_scatter | solution.py:92
  68.0 43.6 %copy-start.2 = (bf16[1,1,128,1024]{3,2,1,0:T(8,128)(2,1)S(1)}, bf16[1,1,128,1024]{3,2,1,0:T(8,128)(2,1)}, u32[]{:S(2)}) copy-start(bf16[1,1,128,1024]{3,2,1,0:T(8,128)(2,1)} %param.13) | copy-start | bytes 786436
  68.0 45.0 %copy-start.14 = (f32[1,1024]{1,0:T(1,128)S(1)}, f32[1,1024]{1,0:T(1,128)}, u32[]{:S(2)}) copy-start(f32[1,1024]{1,0:T(1,128)} %param.17) | copy-start | bytes 12292
  70.1 62.5 %all-gather.11.cloned.1.call-start = ((), (), s32[]{:S(2)}) async-start(), calls=%async_computation.7 | async-start | bytes 4456448 | tf_op jit(solution)/shard_map/all_gather | solution.py:124
  70.7 116.8 %all-gather.15.cloned.1.call-start = ((), (), s32[]{:S(2)}) async-start(), calls=%async_computation.9 | async-start | bytes 2228224 | tf_op jit(solution)/shard_map/all_gather | solution.py:123
  71.3 171.0 %all-gather.17.cloned.1.call-start = ((), (), s32[]{:S(2)}) async-start(), calls=%async_computation.10 | async-start | bytes 2228224 | tf_op jit(solution)/shard_map/all_gather | solution.py:125
  71.9 213.0 %all-gather.9.cloned.1.call-start = ((), (), s32[]{:S(2)}) async-start(), calls=%async_computation.5 | async-start | bytes 2359296 | tf_op jit(solution)/shard_map/all_gather | solution.py:101
  114.0 29.8 %copy-start.12 = (bf16[1,128,1024]{2,1,0:T(8,128)(2,1)S(1)}, bf16[1,128,1024]{2,1,0:T(8,128)(2,1)}, u32[]{:S(2)}) copy-start(bf16[1,128,1024]{2,1,0:T(8,128)(2,1)} %param.20) | copy-start | bytes 786436
  114.0 243.2 %all-gather.13.cloned.1.call-start = ((), (), s32[]{:S(2)}) async-start(), calls=%async_computation.8 | async-start | bytes 4718592 | tf_op jit(solution)/shard_map/all_gather | solution.py:131
  143.8 43.7 %copy-start.8 = (bf16[1,256,1024]{2,1,0:T(8,128)(2,1)S(1)}, bf16[1,256,1024]{2,1,0:T(8,128)(2,1)}, u32[]{:S(2)}) copy-start(bf16[1,256,1024]{2,1,0:T(8,128)(2,1)} %param.21) | copy-start | bytes 1572868
  143.8 98.5 %copy-start.6 = (bf16[1,256,1024]{2,1,0:T(8,128)(2,1)S(1)}, bf16[1,256,1024]{2,1,0:T(8,128)(2,1)}, u32[]{:S(2)}) copy-start(bf16[1,256,1024]{2,1,0:T(8,128)(2,1)} %param.25) | copy-start | bytes 1572868
  148.5 290.5 %reduce-scatter.8.cloned.1.call-start = ((), (), s32[]{:S(2)}) async-start(), calls=%async_computation.6 | async-start | bytes 2359296 | tf_op jit(solution)/shard_map/reduce_scatter | solution.py:109
  290.7 202.2 %reduce-scatter.10.cloned.1.call-start = ((), (), s32[]{:S(2)}) async-start(), calls=%async_computation.12 | async-start | bytes 4718592
  366.6 9.8 %copy-start.4 = (bf16[256,1024]{0,1:T(8,128)(2,1)S(1)}, bf16[256,1024]{0,1:T(8,128)(2,1)}, u32[]{:S(2)}) copy-start(bf16[256,1024]{0,1:T(8,128)(2,1)} %copy.51) | copy-start | bytes 1572868
  422.8 7.1 copy-start.5
  438.8 195.8 %all-reduce.6.cloned.1.call-start = ((), (), s32[]{:S(2)}) async-start(), calls=%async_computation.13 | async-start | bytes 1572864 | tf_op jit(solution)/shard_map/psum | solution.py:18
  495.0 8.8 copy-start.7
  495.0 420.7 %all-reduce.4.cloned.1.call-start = ((), (), s32[]{:S(2)}) async-start(), calls=%async_computation.11 | async-start | bytes 8388608 | tf_op jit(solution)/shard_map/psum | solution.py:161
  506.5 10.0 %copy-start.13 = (bf16[128,1024]{1,0:T(8,128)(2,1)S(1)}, bf16[128,1024]{1,0:T(8,128)(2,1)}, u32[]{:S(2)}) copy-start(bf16[128,1024]{1,0:T(8,128)(2,1)} %get-tuple-element.8) | copy-start | bytes 786436
  506.5 11.9 %copy-start.3 = (bf16[1024,1024]{1,0:T(8,128)(2,1)S(1)}, bf16[1024,1024]{1,0:T(8,128)(2,1)}, u32[]{:S(2)}) copy-start(bf16[1024,1024]{1,0:T(8,128)(2,1)} %all-gather.17.cloned.1.call-done) | copy-start | bytes 6291460
  506.5 11.9 %copy-start.9 = (bf16[1,256,1024]{2,1,0:T(8,128)(2,1)S(1)}, bf16[1,256,1024]{2,1,0:T(8,128)(2,1)}, u32[]{:S(2)}) copy-start(bf16[1,256,1024]{2,1,0:T(8,128)(2,1)} %param.21) | copy-start | bytes 1572868
  516.5 8.2 collective-permute-start
  (3 other events, 15.2 us)
Sparse Core Ops, SparseCore 0:
  12.4 43.7 all-gather.6
  70.3 41.3 reduce-scatter.5
  290.8 69.1 reduce-scatter.7
  439.0 53.9 reduce-scatter.9
Sparse Core Ops, SparseCore 1:
  73.4 59.3 all-gather.10
  135.3 52.1 all-gather.14
  190.1 52.1 all-gather.16
  244.7 40.1 all-gather.8
  286.7 70.4 all-gather.12
  495.1 139.5 all-reduce.5
  640.0 275.7 all-reduce.3
where the time goes:
time: 929 us; the launch traced here: 928 us
  waiting for transfers between devices  738 us (79%)
  matrix products  112 us (12%)
  local copies, waits for them, and re-layouts  49.6 us (5%)
  between operations  15.6 us (2%)
  other arithmetic  10.7 us (1%)
    psum x1, waiting for transfers between devices, local(): out_grad = lax.psum(mix_term, ('section', 'ray', 'dp'))  273 us
    psum x1, waiting for transfers between devices, spread_2(): return lax.psum(jnp.where(mine, value, jnp.zeros_like(value)), axis)  110 us
    all_gather x1, waiting for transfers between devices, local(): lax.all_gather(jnp.dot(latent, flat_pairs, preferred_element_type=jnp.flo...  66.2 us
    unnamed x12, waiting for transfers between devices  53.9 us
    all_gather x1, waiting for transfers between devices, local(): lax.all_gather(dec_out, 'section', axis=0, tiled=True)  51.5 us
    all_gather x1, waiting for transfers between devices, local(): lax.all_gather(normed, 'ray', axis=0, tiled=True)  42.5 us
    reduce_scatter x1, waiting for transfers between devices, local(): lax.psum_scatter(jnp.dot(mixed, w_attn_out, preferred_element_type=jnp.fl...  39.7 us
    all_gather x1, waiting for transfers between devices, local(): lax.all_gather(layer_norm(hidden, gain_two).astype(jnp.bfloat16), 'ray',...  39.2 us
  transfers between devices with their start and end apart: 12, of which 11 were waited for; matrix products, arithmetic and copies ran while one was open for 16% of the time, Pallas kernels for 0%

commit v1 on v0

--- a/solution.py
+++ b/solution.py
@@ -128,12 +128,11 @@
     queries = ray_queries[0]
     cotangent = feature_grad[0]
     flat_pairs = w_pairs.reshape(width, 2 * width)
-    key_values = lax.all_gather(
-        jnp.dot(latent, flat_pairs, preferred_element_type=jnp.float32).astype(jnp.bfloat16),
-        "ray",
-        axis=0,
-        tiled=True,
-    )
+    field = jnp.dot(latent, flat_pairs, preferred_element_type=jnp.float32).astype(jnp.bfloat16)
+    g_now = lax.axis_size("ray")
+    arr_out = jnp.stack([field] * g_now)
+    tall = lax.all_to_all(arr_out, "ray", 0, 0)
+    key_values = jnp.concatenate(tall, 0)
     scene_len = key_values.shape[0]
     ray_rows = queries.shape[0]
     scale = 1.0 / math.sqrt(head_dim)

time: 929 us -> 941 us (1.013)
    all_gather x1 -> x0, waiting for transfers between devices: 66.2 us -> none  [local(): lax.all_gather(jnp.dot(latent, flat_pairs, preferred_element_type=jnp.flo...]
    all_gather x1, waiting for transfers between devices: 18.6 us -> 47.3 us  [local(): lax.all_gather(dec_kv, 'section', axis=0, tiled=True)]
    all_gather x1, waiting for transfers between devices: 39 us -> 64.6 us  [local(): lax.all_gather(dec_query, 'section', axis=0, tiled=True)]
    unnamed x12 -> x11, waiting for transfers between devices: 53.9 us -> 54 us
  transfers between devices with their start and end apart: 12 -> 12, of which waited for: 11 -> 10; matrix products, arithmetic and copies ran while one was open for 16% -> 18% of each run, Pallas kernels for 0% -> 0%
where the time goes in v1:
time: 941 us; the launch traced here: 940 us
  waiting for transfers between devices  735 us (78%)
  matrix products  111 us (12%)
  local copies, waits for them, and re-layouts  58.9 us (6%)
  between operations  14.4 us (2%)
  other arithmetic  10.7 us (1%)
  starting transfers between devices  9.87 us (1%)
    psum x1, waiting for transfers between devices, local(): out_grad = lax.psum(mix_term, ('section', 'ray', 'dp'))  273 us
    psum x1, waiting for transfers between devices, spread_2(): return lax.psum(jnp.where(mine, value, jnp.zeros_like(value)), axis)  111 us
    all_gather x1, waiting for transfers between devices, local(): lax.all_gather(dec_query, 'section', axis=0, tiled=True)  64.6 us
    unnamed x11, waiting for transfers between devices  54 us
    all_gather x1, waiting for transfers between devices, local(): lax.all_gather(dec_out, 'section', axis=0, tiled=True)  51.6 us
    reduce_scatter x1, waiting for transfers between devices, local(): lax.psum_scatter(jnp.dot(mixed, w_attn_out, preferred_element_type=jnp.fl...  48.4 us
    all_gather x1, waiting for transfers between devices, local(): lax.all_gather(dec_kv, 'section', axis=0, tiled=True)  47.3 us
    all_gather x1, waiting for transfers between devices, local(): lax.all_gather(normed, 'ray', axis=0, tiled=True)  41.7 us
  transfers between devices with their start and end apart: 12, of which 10 were waited for; matrix products, arithmetic and copies ran while one was open for 18% of the time, Pallas kernels for 0%

profile of v1, /device:TPU:2, one launch (start us, length us, event | category | flops | bytes accessed | tf_op | source)
XLA Modules:
  0.0 940.1 jit_solution(16832324734643940970)
XLA Ops:
  13.7 41.7 %all-gather.6.cloned.1.call-done = bf16[1024,1024]{1,0:T(8,128)(2,1)} async-done(((bf16[128,1024]{1,0:T(8,128)(2,1)}), bf16[1024,1024]{1,0:T(8,128)(2,1)}) %all-gather.6.cloned.1.call-update) | async-done | bytes 2097168 | tf_op jit(solution)/shard_map/all_gather | solution.py:89
  58.0 4.9 fusion.97
  62.9 4.3 fusion.48
  70.5 47.3 %all-gather.10.cloned.1.call-done = bf16[1024,2,1024]{2,1,0:T(2,128)(2,1)} async-done(((bf16[64,2,1024]{2,1,0:T(2,128)(2,1)}), bf16[1024,2,1024]{2,1,0:T(2,128)(2,1)}) %all-gather.10.cloned.1.call-update) | async-done | bytes 4194320 | tf_op jit(solution)/shard_map/all_gather | solution.py:124
  117.8 11.1 %copy.52 = bf16[1024,2,1024]{0,2,1:T(8,128)(2,1)} copy(bf16[1024,2,1024]{2,1,0:T(2,128)(2,1)} %all-gather.10.cloned.1.call-done) | data formatting | bytes 8388608 | tf_op jit(solution)/shard_map/all_gather | solution.py:124
  135.6 7.1 all-to-all-start
  142.8 48.4 %reduce-scatter.6.cloned.1.call-done = bf16[128,1024]{1,0:T(8,128)(2,1)} async-done(((bf16[1024,1024]{1,0:T(8,128)(2,1)}), bf16[128,1024]{1,0:T(8,128)(2,1)}) %reduce-scatter.6.cloned.1.call-update) | async-done | bytes 262160 | tf_op jit(solution)/shard_map/reduce_scatter | solution.py:92
  193.5 64.6 %all-gather.12.cloned.1.call-done = bf16[1024,1024]{1,0:T(8,128)(2,1)} async-done(((bf16[64,1024]{1,0:T(8,128)(2,1)}), bf16[1024,1024]{1,0:T(8,128)(2,1)}) %all-gather.12.cloned.1.call-update) | async-done | bytes 2097168 | tf_op jit(solution)/shard_map/all_gather | solution.py:123
  261.4 51.6 %all-gather.14.cloned.1.call-done = bf16[1024,1024]{1,0:T(8,128)(2,1)} async-done(((bf16[64,1024]{1,0:T(8,128)(2,1)}), bf16[1024,1024]{1,0:T(8,128)(2,1)}) %all-gather.14.cloned.1.call-update) | async-done | bytes 2097168 | tf_op jit(solution)/shard_map/all_gather | solution.py:125
  316.3 38.9 %all-gather.8.cloned.1.call-done = bf16[1024,1024]{1,0:T(8,128)(2,1)} async-done(((bf16[128,1024]{1,0:T(8,128)(2,1)}), bf16[1024,1024]{1,0:T(8,128)(2,1)}) %all-gather.8.cloned.1.call-update) | async-done | bytes 2097168 | tf_op jit(solution)/shard_map/all_gather | solution.py:101
  355.2 5.8 convolution_convert_fusion.1
  361.3 6.4 copy.54
  377.2 9.9 %fusion.98 = (f32[16,256]{1,0:T(8,128)S(1)}, f32[16,256,1024]{2,1,0:T(8,128)}) fusion(bf16[256,16,64]{0,2,1:T(8,128)(2,1)S(1)} %bitcast.151, bf16[1024,16,64]{0,2,1:T(8,128)(2,1)} %bitcast.146), kind=kOutput, calls=%fused_computation.110 | convolution fusion | flops 549454848 | bytes 19415040 | tf_op jit(solution)/shard_map/sub | solution.py:30
  387.1 8.1 fusion.99
  395.2 38.2 %fusion.38 = bf16[16,64,1024]{2,1,0:T(8,128)(2,1)} fusion(bf16[256,16,64]{0,2,1:T(8,128)(2,1)S(1)} %bitcast.152, f32[16,256,1024]{2,1,0:T(8,128)} %fusion.99, f32[16,256,1024]{2,1,0:T(8,128)} %get-tuple-element.18, f32[16,256]{1,0:T(8,128)S(1)} %get-tuple-element.17), kind=kOutput, calls=%fused_computation.40 | convolution fusion | flops 567284736 | bytes 36192256 | tf_op jit(solution)/shard_map/hrl,rhd->lhd/dot_general | solution.py:169
  433.3 7.1 fusion.35
  442.9 6.5 copy.64
  451.4 52.1 %reduce-scatter.10.cloned.1.call-done = bf16[128,2048]{1,0:T(8,128)(2,1)} async-done(((bf16[1024,2048]{1,0:T(8,128)(2,1)}), bf16[128,2048]{1,0:T(8,128)(2,1)}) %reduce-scatter.10.cloned.1.call-update) | async-done | bytes 524304
  505.8 8.5 fusion.42
  517.1 10.0 %fusion.95 = (bf16[1024,1,1024]{2,1,0:T(2,128)(2,1)}, bf16[1024,1,1024]{2,1,0:T(2,128)(2,1)}) fusion(bf16[1024,2,1024]{2,1,0:T(2,128)(2,1)} %all-gather.10.cloned.1.call-done), kind=kLoop, calls=%fused_computation.107 | loop fusion | bytes 8388608 | tf_op jit(solution)/shard_map/slice | solution.py:49
  530.6 4.5 collective-permute-done
  535.0 111.3 %all-reduce.6.cloned.1.call-done = (bf16[128,1024]{1,0:T(8,128)(2,1)}, bf16[128,2,1024]{0,2,1:T(8,128)(2,1)}) async-done(((bf16[128,1024]{1,0:T(8,128)(2,1)}, bf16[128,2,1024]{0,2,1:T(8,128)(2,1)}), (bf16[128,1024]{1,0:T(8,128)(2,1)}, bf16[128,2,1024]{0,2,1:T(8,128)(2,1)})) %all-reduce.6.cloned.1.call-update) | async-done | bytes 786448 | tf_op jit(solution)/shard_map/psum | solution.py:18
  654.9 272.9 %all-reduce.4.cloned.1.call-done = f32[1024,1024]{1,0:T(8,128)} async-done(((f32[1024,1024]{1,0:T(8,128)}), f32[1024,1024]{1,0:T(8,128)}) %all-reduce.4.cloned.1.call-update) | async-done | bytes 4194320 | tf_op jit(solution)/shard_map/psum | solution.py:160
  928.5 4.8 copy.83
  (86 shorter events, 59.6 us)
Async XLA Ops:
  7.2 348.1 %copy-start = (bf16[1,512,1024]{2,1,0:T(8,128)(2,1)S(1)}, bf16[1,512,1024]{2,1,0:T(8,128)(2,1)}, u32[]{:S(2)}) copy-start(bf16[1,512,1024]{2,1,0:T(8,128)(2,1)} %param.19) | copy-start | bytes 3145732
  7.2 48.2 %all-gather.6.cloned.1.call-start = ((), (), s32[]{:S(2)}) async-start(), calls=%async_computation.4 | async-start | bytes 2359296 | tf_op jit(solution)/shard_map/all_gather | solution.py:89
  11.5 106.4 %all-gather.10.cloned.1.call-start = ((), (), s32[]{:S(2)}) async-start(), calls=%async_computation.8 | async-start | bytes 4456448 | tf_op jit(solution)/shard_map/all_gather | solution.py:124
  12.2 179.0 %reduce-scatter.6.cloned.1.call-start = ((), (), s32[]{:S(2)}) async-start(), calls=%async_computation.5 | async-start | bytes 2359296 | tf_op jit(solution)/shard_map/reduce_scatter | solution.py:92
  69.3 188.8 %all-gather.12.cloned.1.call-start = ((), (), s32[]{:S(2)}) async-start(), calls=%async_computation.9 | async-start | bytes 2228224 | tf_op jit(solution)/shard_map/all_gather | solution.py:123
  69.9 243.1 %all-gather.14.cloned.1.call-start = ((), (), s32[]{:S(2)}) async-start(), calls=%async_computation.10 | async-start | bytes 2228224 | tf_op jit(solution)/shard_map/all_gather | solution.py:125
  70.5 58.5 %copy-start.12 = (bf16[1,128,1024]{2,1,0:T(8,128)(2,1)S(1)}, bf16[1,128,1024]{2,1,0:T(8,128)(2,1)}, u32[]{:S(2)}) copy-start(bf16[1,128,1024]{2,1,0:T(8,128)(2,1)} %param.20) | copy-start | bytes 786436
  135.6 55.6 %copy-start.2 = (bf16[1,1,128,1024]{3,2,1,0:T(8,128)(2,1)S(1)}, bf16[1,1,128,1024]{3,2,1,0:T(8,128)(2,1)}, u32[]{:S(2)}) copy-start(bf16[1,1,128,1024]{3,2,1,0:T(8,128)(2,1)} %param.13) | copy-start | bytes 786436
  135.6 57.0 %copy-start.14 = (f32[1,1024]{1,0:T(1,128)S(1)}, f32[1,1024]{1,0:T(1,128)}, u32[]{:S(2)}) copy-start(f32[1,1024]{1,0:T(1,128)} %param.17) | copy-start | bytes 12292
  135.6 122.5 %copy-start.8 = (bf16[1,256,1024]{2,1,0:T(8,128)(2,1)S(1)}, bf16[1,256,1024]{2,1,0:T(8,128)(2,1)}, u32[]{:S(2)}) copy-start(bf16[1,256,1024]{2,1,0:T(8,128)(2,1)} %param.21) | copy-start | bytes 1572868
  135.6 225.7 %all-to-all-start = ((bf16[8,128,2048]{1,2,0:T(8,128)(2,1)}), bf16[8,128,2048]{1,2,0:T(8,128)(2,1)}, u32[]{:S(2)}, u32[]{:S(2)}) async-start(bf16[8,128,2048]{1,2,0:T(8,128)(2,1)} %stack.5), calls=%async_computation.2 | async-start | bytes 8388608 | tf_op jit(solution)/shard_map/all_to_all | solution.py:134
  142.7 170.3 %copy-start.6 = (bf16[1,256,1024]{2,1,0:T(8,128)(2,1)S(1)}, bf16[1,256,1024]{2,1,0:T(8,128)(2,1)}, u32[]{:S(2)}) copy-start(bf16[1,256,1024]{2,1,0:T(8,128)(2,1)} %param.25) | copy-start | bytes 1572868
  142.7 212.5 %all-gather.8.cloned.1.call-start = ((), (), s32[]{:S(2)}) async-start(), calls=%async_computation.6 | async-start | bytes 2359296 | tf_op jit(solution)/shard_map/all_gather | solution.py:101
  193.5 256.0 %reduce-scatter.8.cloned.1.call-start = ((), (), s32[]{:S(2)}) async-start(), calls=%async_computation.7 | async-start | bytes 2359296 | tf_op jit(solution)/shard_map/reduce_scatter | solution.py:109
  361.1 142.4 %reduce-scatter.10.cloned.1.call-start = ((), (), s32[]{:S(2)}) async-start(), calls=%async_computation.12 | async-start | bytes 4718592
  377.2 9.9 %copy-start.4 = (bf16[256,1024]{0,1:T(8,128)(2,1)S(1)}, bf16[256,1024]{0,1:T(8,128)(2,1)}, u32[]{:S(2)}) copy-start(bf16[256,1024]{0,1:T(8,128)(2,1)} %copy.58) | copy-start | bytes 1572868
  433.3 7.1 copy-start.5
  449.4 196.9 %all-reduce.6.cloned.1.call-start = ((), (), s32[]{:S(2)}) async-start(), calls=%async_computation.13 | async-start | bytes 1572864 | tf_op jit(solution)/shard_map/psum | solution.py:18
  505.6 8.8 copy-start.7
  505.6 422.2 %all-reduce.4.cloned.1.call-start = ((), (), s32[]{:S(2)}) async-start(), calls=%async_computation.11 | async-start | bytes 8388608 | tf_op jit(solution)/shard_map/psum | solution.py:160
  517.1 10.0 %copy-start.13 = (bf16[128,1024]{1,0:T(8,128)(2,1)S(1)}, bf16[128,1024]{1,0:T(8,128)(2,1)}, u32[]{:S(2)}) copy-start(bf16[128,1024]{1,0:T(8,128)(2,1)} %get-tuple-element.8) | copy-start | bytes 786436
  517.1 11.9 %copy-start.3 = (bf16[1024,1024]{1,0:T(8,128)(2,1)S(1)}, bf16[1024,1024]{1,0:T(8,128)(2,1)}, u32[]{:S(2)}) copy-start(bf16[1024,1024]{1,0:T(8,128)(2,1)} %all-gather.14.cloned.1.call-done) | copy-start | bytes 6291460
  517.1 11.9 %copy-start.9 = (bf16[1,256,1024]{2,1,0:T(8,128)(2,1)S(1)}, bf16[1,256,1024]{2,1,0:T(8,128)(2,1)}, u32[]{:S(2)}) copy-start(bf16[1,256,1024]{2,1,0:T(8,128)(2,1)} %param.21) | copy-start | bytes 1572868
  527.1 8.0 collective-permute-start
  (3 other events, 15.2 us)
Sparse Core Ops, SparseCore 0:
  11.6 43.7 all-gather.5
  58.2 59.6 all-gather.9
  120.4 70.7 reduce-scatter.5
  193.8 64.2 all-gather.11
  260.7 52.2 all-gather.13
  315.2 39.9 all-gather.7
  361.2 41.4 reduce-scatter.7
  449.5 53.8 reduce-scatter.9
  506.8 139.5 all-reduce.5
  651.7 276.0 all-reduce.3
